TPU v7x, 32 devices: a whole 2x2x4 slice. The times are simulated.
32 devices in a mesh: row: 4 (over x, core), col: 4 (over z), pt: 2 (over y).
Axes of the slice: x: 2, y: 2, z: 4, core: 2. Of those that a mesh axis runs over, the one named last changes fastest.
Arguments:
- first_factors: int32 [32, 1024, 1024], P('pt', 'row', 'col'), may hold values from 0 to 12288
- second_factors: int32 [32, 1024, 1024], P('pt', 'row', 'col'), may hold values from 0 to 12288
Outputs:
- scaled_product: float32 [45, 1024, 1024], P(None, ('row', 'pt'), 'col')
All inputs are finite; a program needn't handle non-finite values.
Results may differ from a plain program's by a relative error of at most 0.0003.
Values may be sent and summed in bfloat16 or wider, within the bound.
A program may use at most 128 MiB of HBM per device.

v0:
```python
import jax
import jax.numpy as jnp
import numpy as np
from jax import lax
from jax.sharding import PartitionSpec as P

DEG = 16
modulus = 12289
digit_base = 128


def primitive_root():
    for candidate in range(2, modulus):
        if pow(candidate, 6144, modulus) != 1 and pow(candidate, 4096, modulus) != 1:
            return candidate
    return 0


def make_table(order_size, row_count, column_count, inverse):
    generator = primitive_root()
    root_value = pow(generator, (modulus - 1) // order_size, modulus)
    scaling = 1
    if inverse:
        root_value = pow(root_value, modulus - 2, modulus)
        scaling = pow(order_size, modulus - 2, modulus)
    entries = [
        [
            pow(root_value, row_index * column_index % order_size, modulus) * scaling % modulus
            for column_index in range(column_count)
        ]
        for row_index in range(row_count)
    ]
    return np.array(entries, dtype=np.int64)


def value_digits(values):
    high_digit = values // digit_base
    return (
        high_digit.astype(jnp.bfloat16),
        (values - digit_base * high_digit).astype(jnp.bfloat16),
    )


def combine(high_high, high_low, low_high, low_low):
    top_part = high_high.astype(jnp.int32) % modulus
    middle_part = (high_low.astype(jnp.int32) + low_high.astype(jnp.int32)) % modulus
    return (
        top_part * (digit_base * digit_base) % modulus
        + middle_part * digit_base
        + low_low.astype(jnp.int32)
    ) % modulus


def transform(matrix_table, coefs):
    slot_count = coefs.shape[0]
    flat_coefs = coefs.reshape(slot_count, -1)
    table_high = jnp.asarray(matrix_table // digit_base, dtype=jnp.bfloat16)
    table_low = jnp.asarray(matrix_table % digit_base, dtype=jnp.bfloat16)
    data_high, data_low = value_digits(flat_coefs)

    def product_of(left_part, right_part):
        return jnp.dot(left_part, right_part, preferred_element_type=jnp.float32)

    mixed_values = combine(
        product_of(table_high, data_high),
        product_of(table_high, data_low),
        product_of(table_low, data_high),
        product_of(table_low, data_low),
    )
    return mixed_values.reshape(matrix_table.shape[0], coefs.shape[1], coefs.shape[2])


def batched_product(left_part, right_part):
    return jnp.einsum("bik,bkj->bij", left_part, right_part, preferred_element_type=jnp.float32)


def digit_sum(totals, left_digits, right_digits):
    return (
        totals[0] + batched_product(left_digits[0], right_digits[0]),
        totals[1] + batched_product(left_digits[0], right_digits[1]),
        totals[2] + batched_product(left_digits[1], right_digits[0]),
        totals[3] + batched_product(left_digits[1], right_digits[1]),
    )


def pointwise(left_values, right_values):
    left_points, right_points = (
        lax.all_to_all(
            lax.all_to_all(
                left_values.astype(jnp.float32), "col", split_axis=0, concat_axis=2, tiled=True
            ),
            "pt",
            split_axis=0,
            concat_axis=1,
            tiled=True,
        ),
        lax.all_to_all(
            lax.all_to_all(
                right_values.astype(jnp.float32), "col", split_axis=0, concat_axis=2, tiled=True
            ),
            "pt",
            split_axis=0,
            concat_axis=1,
            tiled=True,
        ),
    )
    left_digits = value_digits(left_points.astype(jnp.int32))
    right_digits = value_digits(right_points.astype(jnp.int32))
    zeros_init = jnp.zeros(left_points.shape, jnp.float32)
    column_parts = tuple((digit_part for digit_part in left_digits))
    totals = digit_sum(
        (zeros_init, zeros_init, zeros_init, zeros_init),
        column_parts,
        (
            lax.all_gather(right_digits[0], "row", axis=1, tiled=True),
            lax.all_gather(right_digits[1], "row", axis=1, tiled=True),
        ),
    )
    product_values = combine(totals[0], totals[1], totals[2], totals[3]).astype(jnp.float32)
    arrived = lax.all_to_all(
        lax.all_to_all(product_values, "col", split_axis=2, concat_axis=0, tiled=True),
        "pt",
        split_axis=1,
        concat_axis=0,
        tiled=True,
    )
    col_count = lax.axis_size("col")
    pt_count = lax.axis_size("pt")
    local_count = arrived.shape[0] // (col_count * pt_count)
    returned = arrived.reshape(pt_count, col_count, local_count, arrived.shape[1], arrived.shape[2])
    returned = returned.transpose(1, 0, 2, 3, 4).reshape(arrived.shape)
    return returned.astype(jnp.int32)


def local(first_factors, second_factors):
    forward_one = make_table(2 * DEG, 2 * DEG, DEG, False)
    inverse_one = make_table(2 * DEG, 2 * DEG, 2 * DEG, True)
    forward_two = make_table(4 * DEG, 4 * DEG, 2 * DEG, False)
    inverse_two = make_table(4 * DEG, 3 * DEG - 3, 4 * DEG, True)
    first_entries, second_entries = (
        lax.all_to_all(
            first_factors.astype(jnp.float32), "pt", split_axis=1, concat_axis=0, tiled=True
        ),
        lax.all_to_all(
            second_factors.astype(jnp.float32), "pt", split_axis=1, concat_axis=0, tiled=True
        ),
    )
    first_entries = first_entries.astype(jnp.int32)
    second_entries = second_entries.astype(jnp.int32)
    left_values = jnp.concatenate(
        [transform(forward_one, first_entries[:DEG]), transform(forward_one, first_entries[DEG:])],
        0,
    )
    right_values = jnp.concatenate(
        [
            transform(forward_one, second_entries[:DEG]),
            transform(forward_one, second_entries[DEG:]),
        ],
        0,
    )
    products = pointwise(left_values, right_values)
    first_product = transform(inverse_one, products[: 2 * DEG])
    second_product = transform(inverse_one, products[2 * DEG :])
    upper_values = transform(forward_two, first_product)
    lower_values = transform(forward_two[:, :DEG], second_product[DEG:])
    result_coefficients = transform(inverse_two, pointwise(upper_values, lower_values))
    return result_coefficients.astype(jnp.float32) / 12289.0


def reduce_centred(values):
    return values - 12289.0 * jnp.round(values * (1.0 / 12289.0))


def centred_digits(values):
    high_digit = jnp.round(values * (1.0 / 128.0))
    return (high_digit.astype(jnp.bfloat16), (values - 128.0 * high_digit).astype(jnp.bfloat16))


def combine_centred(high_high, middle, low_low):
    upper_part = reduce_centred(reduce_centred(high_high) * 128.0 + middle)
    return reduce_centred(upper_part * 128.0 + low_low)


def table_digits(matrix_table):
    centred = np.where(matrix_table > modulus // 2, matrix_table - modulus, matrix_table)
    high_digit = np.round(centred / 128.0)
    return (high_digit, centred - 128.0 * high_digit)


def centred_transform(table_high, table_low, coefs):
    data_high, data_low = centred_digits(coefs.astype(jnp.float32))
    table_high = jnp.asarray(table_high, dtype=jnp.bfloat16)
    table_low = jnp.asarray(table_low, dtype=jnp.bfloat16)

    def product_of(left_part, right_part):
        return jnp.einsum("ts,sab->tab", left_part, right_part, preferred_element_type=jnp.float32)

    middle = product_of(
        jnp.concatenate([table_high, table_low], 1), jnp.concatenate([data_low, data_high], 0)
    )
    return combine_centred(
        product_of(table_high, data_high), middle, product_of(table_low, data_low)
    )


def column_pointwise(left_values, right_values):
    right_points = lax.all_to_all(
        right_values.astype(jnp.int16), "col", split_axis=0, concat_axis=2, tiled=True
    )
    right_points = lax.all_gather(right_points, "row", axis=1, tiled=True)
    left_points = lax.all_to_all(
        left_values.astype(jnp.int16), "col", split_axis=0, concat_axis=2, tiled=True
    )
    left_high, left_low = centred_digits(left_points.astype(jnp.float32))
    right_high, right_low = centred_digits(right_points.astype(jnp.float32))
    middle = batched_product(left_high, right_low) + batched_product(left_low, right_high)
    product_values = combine_centred(
        batched_product(left_high, right_high), middle, batched_product(left_low, right_low)
    )
    return lax.all_to_all(
        product_values.astype(jnp.int16), "col", split_axis=2, concat_axis=0, tiled=True
    )


def pair_local(first_factors, second_factors):
    forward_one = table_digits(make_table(2 * DEG, 2 * DEG, DEG, False))
    inverse_one = table_digits(make_table(2 * DEG, 2 * DEG, 2 * DEG, True))
    forward_two = table_digits(make_table(4 * DEG, 4 * DEG, 2 * DEG, False))
    inverse_two = table_digits(make_table(4 * DEG, 3 * DEG - 3, 4 * DEG, True))
    half_points = 2 * DEG
    place = lax.axis_index("pt")
    products = column_pointwise(
        centred_transform(*forward_one, centre(first_factors)),
        centred_transform(*forward_one, centre(second_factors)),
    )
    own_product = centred_transform(*inverse_one, products).astype(jnp.int16)
    both_products = lax.all_gather(own_product, "pt", axis=0, tiled=True)
    first_product = both_products[: 2 * DEG]
    shifted = both_products[3 * DEG :]
    own_tables = [
        lax.dynamic_slice_in_dim(
            jnp.asarray(digit, dtype=jnp.bfloat16), place * half_points, half_points, 0
        )
        for digit in forward_two
    ]
    upper_values = centred_transform(*own_tables, first_product)
    lower_values = centred_transform(*[digit[:, :DEG] for digit in own_tables], shifted)
    products_two = column_pointwise(upper_values, lower_values)
    all_points = lax.all_to_all(products_two, "pt", split_axis=1, concat_axis=0, tiled=True)
    result = centred_transform(*inverse_two, all_points)
    return jnp.where(result < 0.0, result + 12289.0, result) / 12289.0


def centre(values):
    return jnp.where(values > modulus // 2, values - modulus, values)


def solution(mesh):
    in_specs = (P("pt", "row", "col"), P("pt", "row", "col"))
    out_specs = P(None, ("row", "pt"), "col")
    body = pair_local if mesh.shape["pt"] == 2 else local
    return jax.shard_map(body, mesh=mesh, in_specs=in_specs, out_specs=out_specs, check_vma=False)
```

profile of v0, /device:TPU:0, one launch (start us, length us, event | category | flops | bytes accessed | tf_op | source)
XLA Modules:
  0.0 1258.8 jit_solution(4259190581243966023)
XLA Ops:
  45.8 73.8 %all-to-all-done = s16[32,256,256]{2,1,0:T(8,128)(2,1)} async-done(((s16[32,256,256]{2,1,0:T(8,128)(2,1)}), s16[32,256,256]{2,1,0:T(8,128)(2,1)}, u32[]{:S(2)}, u32[]{:S(2)}) %all-to-all-start) | async-done | bytes 4194336 | tf_op jit(solution)/shard_map/all_to_all | solution.py:211
  131.8 12.0 copy.111
  143.8 10.8 reshape.16
  154.6 63.0 %all-to-all-done.1 = s16[32,256,256]{2,1,0:T(8,128)(2,1)} async-done(((s16[32,256,256]{2,1,0:T(8,128)(2,1)}), s16[32,256,256]{2,1,0:T(8,128)(2,1)}, u32[]{:S(2)}, u32[]{:S(2)}) %all-to-all-start.1) | async-done | bytes 4194336 | tf_op jit(solution)/shard_map/all_to_all | solution.py:207
  232.9 105.4 %all-gather.3 = s16[8,1024,1024]{2,1,0:T(8,128)(2,1)} all-gather(s16[8,256,1024]{2,1,0:T(8,128)(2,1)} %all_to_all.71), channel_id=1, replica_groups=mesh['row'=4,'col'=4,'pt'=2] {'row'}, dimensions={1}, use_global_device_ids=true | all-gather | bytes 20971520 | tf_op jit(solution)/shard_map/all_gather | solution.py:210
  338.4 16.5 %fusion.14 = f32[8,256,1024]{2,1,0:T(8,128)} fusion(s16[8,1024,1024]{2,1,0:T(8,128)(2,1)} %all-gather.3, f32[8,256,1024]{2,1,0:T(8,128)} %reshape.16), kind=kOutput, calls=%fused_computation.16 | convolution fusion | flops 4334813184 | bytes 33554432 | tf_op jit(solution)/shard_map/bik,bkj->bij/dot_general | solution.py:74
  354.9 17.6 %fusion.12 = f32[8,256,1024]{2,1,0:T(8,128)} fusion(s16[8,1024,1024]{2,1,0:T(8,128)(2,1)} %all-gather.3, f32[8,256,1024]{2,1,0:T(8,128)} %reshape.16), kind=kOutput, calls=%fused_computation.15 | convolution fusion | flops 4339007488 | bytes 33554432 | tf_op jit(solution)/shard_map/bik,bkj->bij/dot_general | solution.py:74
  372.5 18.3 %fusion.20 = f32[8,256,1024]{2,1,0:T(8,128)} fusion(s16[8,1024,1024]{2,1,0:T(8,128)(2,1)} %all-gather.3, f32[8,256,1024]{2,1,0:T(8,128)} %reshape.16), kind=kOutput, calls=%fused_computation.23 | convolution fusion | flops 4355784704 | bytes 33554432 | tf_op jit(solution)/shard_map/bik,bkj->bij/dot_general | solution.py:74
  390.8 25.6 %subtract_convert_fusion.5 = s16[8,256,1024]{2,1,0:T(8,128)(2,1)} fusion(f32[8,256,1024]{2,1,0:T(8,128)} %fusion.20, f32[8,256,1024]{2,1,0:T(8,128)} %fusion.12, f32[8,256,1024]{2,1,0:T(8,128)} %fusion.14, s16[8,1024,1024]{2,1,0:T(8,128)(2,1)} %all-gather.3, f32[8,256,1024]{2,1,0:T(8,128)} %reshape.16), kind=kOutput, calls=%fused_computation.59 | convolution fusion | flops 4389339136 | bytes 54525952 | tf_op jit(solution)/shard_map/bik,bkj->bij/dot_general | solution.py:74
  428.8 94.0 %all-to-all-done.2 = s16[8,256,1024]{1,0,2:T(8,128)(2,1)} async-done(((s16[8,256,1024]{1,0,2:T(8,128)(2,1)}), s16[8,256,1024]{1,0,2:T(8,128)(2,1)}, u32[]{:S(2)}, u32[]{:S(2)}) %all-to-all-start.2) | async-done | bytes 4194336 | tf_op jit(solution)/shard_map/all_to_all | solution.py:220
  529.3 10.5 copy.77
  555.1 92.8 %all-gather.4 = s16[64,256,256]{2,0,1:T(8,128)(2,1)S(1)} all-gather(s16[32,256,256]{2,0,1:T(8,128)(2,1)} %subtract_convert_fusion.4), channel_id=1, replica_groups=mesh['row'=4,'col'=4,'pt'=2] {'pt'}, dimensions={0}, use_global_device_ids=true | all-gather | bytes 12582912 | tf_op jit(solution)/shard_map/all_gather | solution.py:237
  657.1 10.0 subtract_convert_fusion.3
  698.0 70.7 %all-to-all-done.3 = s16[32,256,256]{2,1,0:T(8,128)(2,1)} async-done(((s16[32,256,256]{2,1,0:T(8,128)(2,1)}), s16[32,256,256]{2,1,0:T(8,128)(2,1)}, u32[]{:S(2)}, u32[]{:S(2)}) %all-to-all-start.3) | async-done | bytes 4194336 | tf_op jit(solution)/shard_map/all_to_all | solution.py:211
  780.6 12.0 copy.110
  792.6 10.8 reshape.18
  803.4 63.1 %all-to-all-done.4 = s16[32,256,256]{2,1,0:T(8,128)(2,1)} async-done(((s16[32,256,256]{2,1,0:T(8,128)(2,1)}), s16[32,256,256]{2,1,0:T(8,128)(2,1)}, u32[]{:S(2)}, u32[]{:S(2)}) %all-to-all-start.4) | async-done | bytes 4194336 | tf_op jit(solution)/shard_map/all_to_all | solution.py:207
  881.9 104.5 %all-gather.5 = s16[8,1024,1024]{2,1,0:T(8,128)(2,1)} all-gather(s16[8,256,1024]{2,1,0:T(8,128)(2,1)} %all_to_all.77), channel_id=1, replica_groups=mesh['row'=4,'col'=4,'pt'=2] {'row'}, dimensions={1}, use_global_device_ids=true | all-gather | bytes 20971520 | tf_op jit(solution)/shard_map/all_gather | solution.py:210
  986.4 16.5 %fusion.10 = f32[8,256,1024]{2,1,0:T(8,128)} fusion(s16[8,1024,1024]{2,1,0:T(8,128)(2,1)} %all-gather.5, f32[8,256,1024]{2,1,0:T(8,128)} %reshape.18), kind=kOutput, calls=%fused_computation.14 | convolution fusion | flops 4334813184 | bytes 33554432 | tf_op jit(solution)/shard_map/bik,bkj->bij/dot_general | solution.py:74
  1002.9 17.6 %fusion.8 = f32[8,256,1024]{2,1,0:T(8,128)} fusion(s16[8,1024,1024]{2,1,0:T(8,128)(2,1)} %all-gather.5, f32[8,256,1024]{2,1,0:T(8,128)} %reshape.18), kind=kOutput, calls=%fused_computation.13 | convolution fusion | flops 4339007488 | bytes 33554432 | tf_op jit(solution)/shard_map/bik,bkj->bij/dot_general | solution.py:74
  1020.5 18.3 %fusion.16 = f32[8,256,1024]{2,1,0:T(8,128)} fusion(s16[8,1024,1024]{2,1,0:T(8,128)(2,1)} %all-gather.5, f32[8,256,1024]{2,1,0:T(8,128)} %reshape.18), kind=kOutput, calls=%fused_computation.21 | convolution fusion | flops 4355784704 | bytes 33554432 | tf_op jit(solution)/shard_map/bik,bkj->bij/dot_general | solution.py:74
  1038.7 25.6 %subtract_convert_fusion = s16[8,256,1024]{2,1,0:T(8,128)(2,1)} fusion(f32[8,256,1024]{2,1,0:T(8,128)} %fusion.16, f32[8,256,1024]{2,1,0:T(8,128)} %fusion.8, f32[8,256,1024]{2,1,0:T(8,128)} %fusion.10, s16[8,1024,1024]{2,1,0:T(8,128)(2,1)} %all-gather.5, f32[8,256,1024]{2,1,0:T(8,128)} %reshape.18), kind=kOutput, calls=%fused_computation.52 | convolution fusion | flops 4389339136 | bytes 54525952 | tf_op jit(solution)/shard_map/bik,bkj->bij/dot_general | solution.py:74
  1071.5 99.7 %all_to_all.90 = s16[8,256,1024]{1,0,2:T(8,128)(2,1)} all-to-all(s16[8,256,1024]{1,0,2:T(8,128)(2,1)} %copy.84), channel_id=1, replica_groups=mesh['row'=4,'col'=4,'pt'=2] {'col'}, dimensions={2} | all-to-all | bytes 8388608 | tf_op jit(solution)/shard_map/all_to_all | solution.py:220
  1183.6 50.0 %all_to_all.91 = s16[32,256,256]{2,0,1:T(8,128)(2,1)S(1)} all-to-all(s16[32,256,256]{2,0,1:T(8,128)(2,1)S(1)} %copy.87), channel_id=1, replica_groups=mesh['row'=4,'col'=4,'pt'=2] {'pt'}, dimensions={1} | all-to-all | bytes 8388608 | tf_op jit(solution)/shard_map/all_to_all | solution.py:249
  (78 shorter events, 219.2 us)
Async XLA Ops:
  0.0 5.5 copy-start.3
  0.0 6.8 copy-start.2
  6.7 1.4 copy-start.11
  19.6 100.0 %all-to-all-start = ((s16[32,256,256]{2,1,0:T(8,128)(2,1)}), s16[32,256,256]{2,1,0:T(8,128)(2,1)}, u32[]{:S(2)}, u32[]{:S(2)}) async-start(s16[32,256,256]{2,1,0:T(8,128)(2,1)} %copy.69), calls=%async_computation | async-start | bytes 8388608 | tf_op jit(solution)/shard_map/all_to_all | solution.py:211
  119.6 98.0 %all-to-all-start.1 = ((s16[32,256,256]{2,1,0:T(8,128)(2,1)}), s16[32,256,256]{2,1,0:T(8,128)(2,1)}, u32[]{:S(2)}, u32[]{:S(2)}) async-start(s16[32,256,256]{2,1,0:T(8,128)(2,1)} %copy.74), calls=%async_computation.1 | async-start | bytes 8388608 | tf_op jit(solution)/shard_map/all_to_all | solution.py:207
  416.3 12.5 copy-start.1
  416.3 12.5 copy-start.4
  423.6 99.2 %all-to-all-start.2 = ((s16[8,256,1024]{1,0,2:T(8,128)(2,1)}), s16[8,256,1024]{1,0,2:T(8,128)(2,1)}, u32[]{:S(2)}, u32[]{:S(2)}) async-start(s16[8,256,1024]{1,0,2:T(8,128)(2,1)} %copy.76), calls=%async_computation.2 | async-start | bytes 8388608 | tf_op jit(solution)/shard_map/all_to_all | solution.py:220
  539.8 4.5 copy-start.8
  544.3 1.3 copy-start.7
  545.5 1.5 copy-start.10
  648.0 9.1 copy-start
  671.3 97.4 %all-to-all-start.3 = ((s16[32,256,256]{2,1,0:T(8,128)(2,1)}), s16[32,256,256]{2,1,0:T(8,128)(2,1)}, u32[]{:S(2)}, u32[]{:S(2)}) async-start(s16[32,256,256]{2,1,0:T(8,128)(2,1)} %copy.78), calls=%async_computation.3 | async-start | bytes 8388608 | tf_op jit(solution)/shard_map/all_to_all | solution.py:211
  676.4 4.3 slice-start
  679.4 2.2 slice-start.1
  768.7 97.8 %all-to-all-start.4 = ((s16[32,256,256]{2,1,0:T(8,128)(2,1)}), s16[32,256,256]{2,1,0:T(8,128)(2,1)}, u32[]{:S(2)}, u32[]{:S(2)}) async-start(s16[32,256,256]{2,1,0:T(8,128)(2,1)} %copy.82), calls=%async_computation.4 | async-start | bytes 8388608 | tf_op jit(solution)/shard_map/all_to_all | solution.py:207
  1242.3 2.2 copy-start.5
  1244.4 1.0 copy-start.6
  1245.4 1.5 copy-start.9
where the time goes:
time: 1270 us; the launch traced here: 1260 us
  blocking collectives  452 us (36%)
  waiting for transfers between devices  364 us (29%)
  matrix products  221 us (17%)
  local copies, waits for them, and re-layouts  148 us (12%)
  other arithmetic  45.2 us (4%)
  starting transfers between devices  27.2 us (2%)
    all_gather x2, blocking collectives, column_pointwise(): right_points = lax.all_gather(right_points, 'row', axis=1, tiled=True)  210 us
    dot_general x8, matrix products, batched_product(): jnp.einsum('bik,bkj->bij', left_part, right_part, preferred_element_type=...  156 us
    all_to_all x2, waiting for transfers between devices, column_pointwise(): lax.all_to_all(left_values.astype(jnp.int16), 'col', split_axis=0, concat...  144 us
    all_to_all x2, waiting for transfers between devices, column_pointwise(): lax.all_to_all(right_values.astype(jnp.int16), 'col', split_axis=0, conca...  126 us
    all_to_all x1, blocking collectives, column_pointwise(): lax.all_to_all(product_values.astype(jnp.int16), 'col', split_axis=2, con...  99.7 us
    all_to_all x1, waiting for transfers between devices, column_pointwise(): lax.all_to_all(product_values.astype(jnp.int16), 'col', split_axis=2, con...  94 us
    all_gather x1, blocking collectives, pair_local(): both_products = lax.all_gather(own_product, 'pt', axis=0, tiled=True)  92.8 us
    dot_general x18, matrix products, product_of(): jnp.einsum('ts,sab->tab', left_part, right_part, preferred_element_type=j...  65.3 us
  transfers between devices with their start and end apart: 5, of which 5 were waited for; matrix products, arithmetic and copies ran while one was open for 8% of the time, Pallas kernels for 0%

commit v1 on v0

--- a/solution.py
+++ b/solution.py
@@ -204,9 +204,20 @@
 
 
 def column_pointwise(left_values, right_values):
-    right_points = lax.all_to_all(
-        right_values.astype(jnp.int16), "col", split_axis=0, concat_axis=2, tiled=True
-    )
+    value = right_values.astype(jnp.int16)
+    ways, here = (lax.axis_size("col"), lax.axis_index("col"))
+    width = value.shape[0] // ways
+    lengths = list(value.shape)
+    lengths[0] = width
+    height = lengths[2]
+    lengths[2] = height * ways
+    full = jnp.zeros(lengths, value.dtype)
+    for mask in range(ways):
+        part = lax.dynamic_slice_in_dim(value, (here ^ mask) * width, width, axis=0)
+        if mask:
+            part = lax.ppermute(part, "col", [(d, d ^ mask) for d in range(ways)])
+        full = lax.dynamic_update_slice_in_dim(full, part, (here ^ mask) * height, axis=2)
+    right_points = full
     right_points = lax.all_gather(right_points, "row", axis=1, tiled=True)
     left_points = lax.all_to_all(
         left_values.astype(jnp.int16), "col", split_axis=0, concat_axis=2, tiled=True

time: 1270 us -> 1170 us (0.921)
  waiting for transfers between devices: 364 us -> 228 us
  starting transfers between devices: 27.2 us -> 66.6 us
  local copies, waits for them, and re-layouts: 148 us -> 123 us
  blocking collectives: 452 us -> 476 us
    all_to_all x2, waiting for transfers between devices: 144 us -> 0.01 us  [column_pointwise(): lax.all_to_all(left_values.astype(jnp.int16), 'col', split_axis=0, concat...]
    ppermute x0 -> x6, waiting for transfers between devices: none -> 133 us  [column_pointwise(): part = lax.ppermute(part, 'col', [(d, d ^ mask) for d in range(ways)])]
    all_to_all x2 -> x0, waiting for transfers between devices: 126 us -> none  [column_pointwise(): lax.all_to_all(right_values.astype(jnp.int16), 'col', split_axis=0, conca...]
    all_to_all x1, starting transfers between devices: 5.15 us -> 46.4 us  [column_pointwise(): lax.all_to_all(product_values.astype(jnp.int16), 'col', split_axis=2, con...]
    all_to_all x1, blocking collectives: 99.7 us -> 140 us  [column_pointwise(): lax.all_to_all(product_values.astype(jnp.int16), 'col', split_axis=2, con...]
    all_to_all x4 -> x0, local copies, waits for them, and re-layouts: 30.7 us -> none  [column_pointwise(): lax.all_to_all(right_values.astype(jnp.int16), 'col', split_axis=0, conca...]
    all_gather x2, blocking collectives: 210 us -> 191 us  [column_pointwise(): right_points = lax.all_gather(right_points, 'row', axis=1, tiled=True)]
  transfers between devices with their start and end apart: 5 -> 9, of which waited for: 5 -> 5; matrix products, arithmetic and copies ran while one was open for 8% -> 4% of each run, Pallas kernels for 0% -> 0%
where the time goes in v1:
time: 1170 us
  blocking collectives  476 us (41%)
  matrix products  232 us (20%)
  waiting for transfers between devices  228 us (19%)
  local copies, waits for them, and re-layouts  123 us (11%)
  starting transfers between devices  66.6 us (6%)
  other arithmetic  42.6 us (4%)
    all_gather x2, blocking collectives, column_pointwise(): right_points = lax.all_gather(right_points, 'row', axis=1, tiled=True)  191 us
    dot_general x8, matrix products, batched_product(): jnp.einsum('bik,bkj->bij', left_part, right_part, preferred_element_type=...  161 us
    all_to_all x1, blocking collectives, column_pointwise(): lax.all_to_all(product_values.astype(jnp.int16), 'col', split_axis=2, con...  140 us
    ppermute x6, waiting for transfers between devices, column_pointwise(): part = lax.ppermute(part, 'col', [(d, d ^ mask) for d in range(ways)])  133 us
    all_to_all x1, waiting for transfers between devices, column_pointwise(): lax.all_to_all(product_values.astype(jnp.int16), 'col', split_axis=2, con...  94.6 us
    all_gather x1, blocking collectives, pair_local(): both_products = lax.all_gather(own_product, 'pt', axis=0, tiled=True)  93.4 us
    dot_general x18, matrix products, product_of(): jnp.einsum('ts,sab->tab', left_part, right_part, preferred_element_type=j...  70.9 us
    all_to_all x1, blocking collectives, pair_local(): lax.all_to_all(products_two, 'pt', split_axis=1, concat_axis=0, tiled=True)  50.8 us
  transfers between devices with their start and end apart: 9, of which 5 were waited for; matrix products, arithmetic and copies ran while one was open for 4% of the time, Pallas kernels for 0%

profile of v1, /device:TPU:0, one launch (start us, length us, event | category | flops | bytes accessed | tf_op | source)
XLA Modules:
  0.0 1168.8 jit_solution(11263585071370423219)
XLA Ops:
  48.0 19.8 %collective-permute-done = s16[8,256,256]{2,0,1:T(8,128)(2,1)} collective-permute-done((s16[8,256,256]{2,0,1:T(8,128)(2,1)}, s16[8,256,256]{2,0,1:T(8,128)(2,1)}, u32[]{:S(2)}, u32[]{:S(2)}) %collective-permute-start) | collective-permute-done | bytes 1048608 | tf_op jit(solution)/shard_map/ppermute | solution.py:218
  69.4 46.8 %collective-permute-done.1 = s16[8,256,256]{2,0,1:T(8,128)(2,1)} collective-permute-done((s16[8,256,256]{2,0,1:T(8,128)(2,1)S(1)}, s16[8,256,256]{2,0,1:T(8,128)(2,1)}, u32[]{:S(2)}, u32[]{:S(2)}) %collective-permute-start.1) | collective-permute-done | bytes 1048608 | tf_op jit(solution)/shard_map/ppermute | solution.py:218
  119.3 96.1 %all-gather.3 = s16[8,1024,1024]{2,1,0:T(8,128)(2,1)} all-gather(s16[8,256,1024]{2,1,0:T(8,128)(2,1)S(1)} %copy_dynamic-update-slice_fusion.4), channel_id=1, replica_groups=mesh['row'=4,'col'=4,'pt'=2] {'row'}, dimensions={1}, use_global_device_ids=true | all-gather | bytes 20971520 | tf_op jit(solution)/shard_map/all_gather | solution.py:221
  222.2 12.0 %copy.137 = f32[4,8,256,256]{3,0,2,1:T(4,128)} copy(f32[4,8,256,256]{3,2,1,0:T(8,128)} %convert.12) | data formatting | bytes 16777216 | tf_op jit(solution)/shard_map/convert_element_type | solution.py:225
  234.2 11.2 reshape.16
  245.5 16.5 %fusion.14 = f32[8,256,1024]{2,1,0:T(8,128)} fusion(s16[8,1024,1024]{2,1,0:T(8,128)(2,1)} %all-gather.3, f32[8,256,1024]{2,1,0:T(8,128)} %reshape.16), kind=kOutput, calls=%fused_computation.16 | convolution fusion | flops 4334813184 | bytes 33554432 | tf_op jit(solution)/shard_map/bik,bkj->bij/dot_general | solution.py:74
  262.0 17.6 %fusion.12 = f32[8,256,1024]{2,1,0:T(8,128)} fusion(s16[8,1024,1024]{2,1,0:T(8,128)(2,1)} %all-gather.3, f32[8,256,1024]{2,1,0:T(8,128)} %reshape.16), kind=kOutput, calls=%fused_computation.15 | convolution fusion | flops 4339007488 | bytes 33554432 | tf_op jit(solution)/shard_map/bik,bkj->bij/dot_general | solution.py:74
  279.6 18.9 %fusion.22 = f32[8,256,1024]{2,1,0:T(8,128)} fusion(s16[8,1024,1024]{2,1,0:T(8,128)(2,1)} %all-gather.3, f32[8,256,1024]{2,1,0:T(8,128)} %reshape.16), kind=kOutput, calls=%fused_computation.24 | convolution fusion | flops 4351590400 | bytes 33554432 | tf_op jit(solution)/shard_map/bik,bkj->bij/dot_general | solution.py:74
  298.5 27.5 %subtract_convert_fusion.5 = s16[8,256,1024]{2,1,0:T(8,128)(2,1)} fusion(f32[8,256,1024]{2,1,0:T(8,128)} %fusion.22, f32[8,256,1024]{2,1,0:T(8,128)} %fusion.12, f32[8,256,1024]{2,1,0:T(8,128)} %fusion.14, s16[8,1024,1024]{2,1,0:T(8,128)(2,1)} %all-gather.3, f32[8,256,1024]{2,1,0:T(8,128)} %reshape.16), kind=kOutput, calls=%fused_computation.59 | convolution fusion | flops 4393533440 | bytes 54525952 | tf_op jit(solution)/shard_map/bik,bkj->bij/dot_general | solution.py:74
  333.2 46.4 %all-to-all-start.1 = ((s16[8,256,1024]{1,0,2:T(8,128)(2,1)}), s16[8,256,1024]{1,0,2:T(8,128)(2,1)}, u32[]{:S(2)}, u32[]{:S(2)}) async-start(s16[8,256,1024]{1,0,2:T(8,128)(2,1)} %copy.94), calls=%async_computation.1 | async-start | bytes 8388608 | tf_op jit(solution)/shard_map/all_to_all | solution.py:231
  379.7 94.6 %all-to-all-done.1 = s16[8,256,1024]{1,0,2:T(8,128)(2,1)} async-done(((s16[8,256,1024]{1,0,2:T(8,128)(2,1)}), s16[8,256,1024]{1,0,2:T(8,128)(2,1)}, u32[]{:S(2)}, u32[]{:S(2)}) %all-to-all-start.1) | async-done | bytes 4194336 | tf_op jit(solution)/shard_map/all_to_all | solution.py:231
  480.8 10.5 copy.95
  506.7 93.4 %all-gather.4 = s16[64,256,256]{2,0,1:T(8,128)(2,1)S(1)} all-gather(s16[32,256,256]{2,0,1:T(8,128)(2,1)} %subtract_convert_fusion.4), channel_id=1, replica_groups=mesh['row'=4,'col'=4,'pt'=2] {'pt'}, dimensions={0}, use_global_device_ids=true | all-gather | bytes 12582912 | tf_op jit(solution)/shard_map/all_gather | solution.py:248
  655.7 22.0 %collective-permute-done.3 = s16[8,256,256]{2,0,1:T(8,128)(2,1)} collective-permute-done((s16[8,256,256]{2,0,1:T(8,128)(2,1)}, s16[8,256,256]{2,0,1:T(8,128)(2,1)}, u32[]{:S(2)}, u32[]{:S(2)}) %collective-permute-start.3) | collective-permute-done | bytes 1048608 | tf_op jit(solution)/shard_map/ppermute | solution.py:218
  679.3 44.9 %collective-permute-done.4 = s16[8,256,256]{2,0,1:T(8,128)(2,1)} collective-permute-done((s16[8,256,256]{2,0,1:T(8,128)(2,1)}, s16[8,256,256]{2,0,1:T(8,128)(2,1)}, u32[]{:S(2)}, u32[]{:S(2)}) %collective-permute-start.4) | collective-permute-done | bytes 1048608 | tf_op jit(solution)/shard_map/ppermute | solution.py:218
  727.4 95.2 %all-gather.5 = s16[8,1024,1024]{2,1,0:T(8,128)(2,1)} all-gather(s16[8,256,1024]{2,1,0:T(8,128)(2,1)S(1)} %copy_dynamic-update-slice_fusion), channel_id=1, replica_groups=mesh['row'=4,'col'=4,'pt'=2] {'row'}, dimensions={1}, use_global_device_ids=true | all-gather | bytes 20971520 | tf_op jit(solution)/shard_map/all_gather | solution.py:221
  829.4 12.0 %copy.136 = f32[4,8,256,256]{3,0,2,1:T(4,128)} copy(f32[4,8,256,256]{3,2,1,0:T(8,128)} %convert.14) | data formatting | bytes 16777216 | tf_op jit(solution)/shard_map/convert_element_type | solution.py:225
  841.4 11.2 reshape.18
  852.6 16.5 %fusion.10 = f32[8,256,1024]{2,1,0:T(8,128)} fusion(s16[8,1024,1024]{2,1,0:T(8,128)(2,1)} %all-gather.5, f32[8,256,1024]{2,1,0:T(8,128)} %reshape.18), kind=kOutput, calls=%fused_computation.14 | convolution fusion | flops 4334813184 | bytes 33554432 | tf_op jit(solution)/shard_map/bik,bkj->bij/dot_general | solution.py:74
  869.1 17.6 %fusion.8 = f32[8,256,1024]{2,1,0:T(8,128)} fusion(s16[8,1024,1024]{2,1,0:T(8,128)(2,1)} %all-gather.5, f32[8,256,1024]{2,1,0:T(8,128)} %reshape.18), kind=kOutput, calls=%fused_computation.13 | convolution fusion | flops 4339007488 | bytes 33554432 | tf_op jit(solution)/shard_map/bik,bkj->bij/dot_general | solution.py:74
  886.7 18.9 %fusion.18 = f32[8,256,1024]{2,1,0:T(8,128)} fusion(s16[8,1024,1024]{2,1,0:T(8,128)(2,1)} %all-gather.5, f32[8,256,1024]{2,1,0:T(8,128)} %reshape.18), kind=kOutput, calls=%fused_computation.22 | convolution fusion | flops 4351590400 | bytes 33554432 | tf_op jit(solution)/shard_map/bik,bkj->bij/dot_general | solution.py:74
  905.6 27.5 %subtract_convert_fusion = s16[8,256,1024]{2,1,0:T(8,128)(2,1)} fusion(f32[8,256,1024]{2,1,0:T(8,128)} %fusion.18, f32[8,256,1024]{2,1,0:T(8,128)} %fusion.8, f32[8,256,1024]{2,1,0:T(8,128)} %fusion.10, s16[8,1024,1024]{2,1,0:T(8,128)(2,1)} %all-gather.5, f32[8,256,1024]{2,1,0:T(8,128)} %reshape.18), kind=kOutput, calls=%fused_computation.52 | convolution fusion | flops 4393533440 | bytes 54525952 | tf_op jit(solution)/shard_map/bik,bkj->bij/dot_general | solution.py:74
  940.3 140.3 %all_to_all.54 = s16[8,256,1024]{1,0,2:T(8,128)(2,1)} all-to-all(s16[8,256,1024]{1,0,2:T(8,128)(2,1)} %copy.104), channel_id=1, replica_groups=mesh['row'=4,'col'=4,'pt'=2] {'col'}, dimensions={2} | all-to-all | bytes 8388608 | tf_op jit(solution)/shard_map/all_to_all | solution.py:231
  1093.0 50.8 %all_to_all.55 = s16[32,256,256]{2,0,1:T(8,128)(2,1)S(1)} all-to-all(s16[32,256,256]{2,0,1:T(8,128)(2,1)S(1)} %copy.107), channel_id=1, replica_groups=mesh['row'=4,'col'=4,'pt'=2] {'pt'}, dimensions={1} | all-to-all | bytes 8388608 | tf_op jit(solution)/shard_map/all_to_all | solution.py:260
  (91 shorter events, 200.0 us)
Async XLA Ops:
  0.0 6.8 copy-start.5
  0.0 8.1 copy-start.4
  6.8 1.6 copy-start
  8.1 1.9 copy-start.13
  17.0 7.2 copy-start.2
  18.6 49.2 %collective-permute-start = (s16[8,256,256]{2,0,1:T(8,128)(2,1)}, s16[8,256,256]{2,0,1:T(8,128)(2,1)}, u32[]{:S(2)}, u32[]{:S(2)}) collective-permute-start(s16[8,256,256]{2,0,1:T(8,128)(2,1)} %get-tuple-element.21), channel_id=1, source_target_pairs={{0,2},{2,0},{4,6},{6,4},{1,3},{3,1},{5,7},{7,5},{8,10},{10,8},{12,... | collective-permute-start | bytes 3145736 | tf_op jit(solution)/shard_map/ppermute | solution.py:218
  21.7 94.5 %collective-permute-start.1 = (s16[8,256,256]{2,0,1:T(8,128)(2,1)S(1)}, s16[8,256,256]{2,0,1:T(8,128)(2,1)}, u32[]{:S(2)}, u32[]{:S(2)}) collective-permute-start(s16[8,256,256]{2,0,1:T(8,128)(2,1)S(1)} %get-tuple-element.20), channel_id=1, source_target_pairs={{0,4},{2,6},{4,0},{6,2},{1,5},{3,7},{5,1},{7,3},{8,12},{10,14},{12... | collective-permute-start | bytes 3145736 | tf_op jit(solution)/shard_map/ppermute | solution.py:218
  24.2 93.5 %collective-permute-start.2 = (s16[8,256,256]{2,0,1:T(8,128)(2,1)S(1)}, s16[8,256,256]{2,0,1:T(8,128)(2,1)}, u32[]{:S(2)}, u32[]{:S(2)}) collective-permute-start(s16[8,256,256]{2,0,1:T(8,128)(2,1)S(1)} %get-tuple-element.19), channel_id=1, source_target_pairs={{0,6},{2,4},{4,2},{6,0},{1,7},{3,5},{5,3},{7,1},{8,14},{10,12},{12... | collective-permute-start | bytes 3145736 | tf_op jit(solution)/shard_map/ppermute | solution.py:218
  42.0 173.4 %all-to-all-start = ((s16[32,256,256]{2,1,0:T(8,128)(2,1)}), s16[32,256,256]{2,1,0:T(8,128)(2,1)}, u32[]{:S(2)}, u32[]{:S(2)}) async-start(s16[32,256,256]{2,1,0:T(8,128)(2,1)} %copy.85), calls=%async_computation | async-start | bytes 8388608 | tf_op jit(solution)/shard_map/all_to_all | solution.py:222
  325.9 53.7 %copy-start.3 = (bf16[64,32]{1,0:T(8,128)(2,1)S(1)}, bf16[64,32]{1,0:T(8,128)(2,1)}, u32[]{:S(2)}) copy-start(bf16[64,32]{1,0:T(8,128)(2,1)} %constant.24.clone) | copy-start | bytes 12292
  325.9 53.8 %copy-start.6 = (bf16[64,32]{1,0:T(8,128)(2,1)S(1)}, bf16[64,32]{1,0:T(8,128)(2,1)}, u32[]{:S(2)}) copy-start(bf16[64,32]{1,0:T(8,128)(2,1)} %constant.23.clone) | copy-start | bytes 12292
  333.2 141.1 %all-to-all-start.1 = ((s16[8,256,1024]{1,0,2:T(8,128)(2,1)}), s16[8,256,1024]{1,0,2:T(8,128)(2,1)}, u32[]{:S(2)}, u32[]{:S(2)}) async-start(s16[8,256,1024]{1,0,2:T(8,128)(2,1)} %copy.94), calls=%async_computation.1 | async-start | bytes 8388608 | tf_op jit(solution)/shard_map/all_to_all | solution.py:231
  491.3 4.5 copy-start.10
  495.8 1.3 copy-start.9
  497.1 1.5 copy-start.12
  629.5 48.2 %collective-permute-start.3 = (s16[8,256,256]{2,0,1:T(8,128)(2,1)}, s16[8,256,256]{2,0,1:T(8,128)(2,1)}, u32[]{:S(2)}, u32[]{:S(2)}) collective-permute-start(s16[8,256,256]{2,0,1:T(8,128)(2,1)} %get-tuple-element.15), channel_id=1, source_target_pairs={{0,2},{2,0},{4,6},{6,4},{1,3},{3,1},{5,7},{7,5},{8,10},{10,8},{12,... | collective-permute-start | bytes 3145736 | tf_op jit(solution)/shard_map/ppermute | solution.py:218
  629.5 94.7 %collective-permute-start.4 = (s16[8,256,256]{2,0,1:T(8,128)(2,1)}, s16[8,256,256]{2,0,1:T(8,128)(2,1)}, u32[]{:S(2)}, u32[]{:S(2)}) collective-permute-start(s16[8,256,256]{2,0,1:T(8,128)(2,1)} %get-tuple-element.14), channel_id=1, source_target_pairs={{0,4},{2,6},{4,0},{6,2},{1,5},{3,7},{5,1},{7,3},{8,12},{10,14},{12... | collective-permute-start | bytes 3145736 | tf_op jit(solution)/shard_map/ppermute | solution.py:218
  631.5 94.3 %collective-permute-start.5 = (s16[8,256,256]{2,0,1:T(8,128)(2,1)}, s16[8,256,256]{2,0,1:T(8,128)(2,1)}, u32[]{:S(2)}, u32[]{:S(2)}) collective-permute-start(s16[8,256,256]{2,0,1:T(8,128)(2,1)} %get-tuple-element.13), channel_id=1, source_target_pairs={{0,6},{2,4},{4,2},{6,0},{1,7},{3,5},{5,3},{7,1},{8,14},{10,12},{12... | collective-permute-start | bytes 3145736 | tf_op jit(solution)/shard_map/ppermute | solution.py:218
  649.8 5.6 copy-start.1
  649.8 172.8 %all-to-all-start.2 = ((s16[32,256,256]{2,1,0:T(8,128)(2,1)}), s16[32,256,256]{2,1,0:T(8,128)(2,1)}, u32[]{:S(2)}, u32[]{:S(2)}) async-start(s16[32,256,256]{2,1,0:T(8,128)(2,1)} %copy.96), calls=%async_computation.2 | async-start | bytes 8388608 | tf_op jit(solution)/shard_map/all_to_all | solution.py:222
  1152.4 2.2 copy-start.7
  1154.6 1.0 copy-start.8
  1155.6 1.5 copy-start.11
